TPU v7x, 256 devices: a whole 4x4x8 slice. The times are simulated.
256 devices in a mesh: dp: 8 (over x, core), vocab: 32 (over z, y).
Axes of the slice: x: 4, y: 4, z: 8, core: 2. Of those that a mesh axis runs over, the one named last changes fastest.
Arguments:
- hidden: bfloat16 [1024, 8192], P('dp', 'vocab'), may hold values from -500 to 500, as said below
- norm_gain: float32 [8192], replicated, may hold values from 0.5 to 1.5
- head_weight: bfloat16 [65536, 8192], P('vocab', 'dp'), may hold values from -1 to 1
- target_logits: bfloat16 [1024, 65536], P('dp', 'vocab'), may hold values from -20 to 400
- valid_rows: int32 [1024], P('dp'), may hold values from 0 to 1, as said below
- parents: int32 [1024], P('dp'), may hold values from 0 to 62, as said below
- features: bfloat16 [1024, 24576], P('dp', 'vocab'), may hold values from -0.29882812 to 0.29882812
Outputs:
- grad_hidden: bfloat16 [1024, 8192], P('vocab', 'dp')
- grad_joining: float32 [8192, 24576], P('dp', 'vocab')
Inputs may be any that keep to these rules, and one draw needn't show every extreme that they name: hidden is finite; in some draws a few rows are far from the others. `valid_rows`: row 0 is always valid. `parents`: rows form trees of 64 rows aligned on multiples of 64; a tree's first row has parent 0, every other row a parent before it in its tree, and the last row of each tree has parent 64 - 2.
All inputs are finite; a program needn't handle non-finite values.
Results may differ from a plain program's by a relative error of at most 0.007.
Values may be sent and summed in bfloat16 or wider, within the bound.
A program may use at most 64 MiB of HBM per device.

v0:
```python
import jax
import jax.numpy as jnp
from jax import lax
from jax.sharding import PartitionSpec as P

TREE = 64


def row_logits(normed_rows, head_weight):
    return lax.dot_general(
        normed_rows, head_weight, (((1,), (1,)), ((), ())), preferred_element_type=jnp.float32
    )


def body(hidden, norm_gain, head_weight, target_logits, valid_rows, parents, features):
    group_index = lax.axis_index("dp")
    vocab_index = lax.axis_index("vocab")
    group_rows = hidden.shape[0]
    whole_rows = lax.all_gather(hidden, "vocab", axis=1, tiled=True)
    model_width = whole_rows.shape[1]
    slice_rows = lax.all_to_all(whole_rows, "dp", split_axis=1, concat_axis=0, tiled=True)
    all_rows = slice_rows.shape[0]
    slice_width = slice_rows.shape[1]
    share_rows = all_rows // lax.axis_size("vocab")
    gain_slice = lax.dynamic_slice_in_dim(norm_gain, group_index * slice_width, slice_width)
    live_rows = (valid_rows == 1).astype(jnp.float32)
    square_part = jnp.sum(jnp.square(slice_rows.astype(jnp.float32)), axis=1)
    squares, valid_count = lax.psum((square_part, jnp.sum(live_rows)), "dp")
    row_factor = lax.rsqrt(squares / model_width + 1e-05)
    normed = (slice_rows.astype(jnp.float32) * row_factor[:, None] * gain_slice).astype(
        jnp.bfloat16
    )
    logits = lax.psum_scatter(
        row_logits(normed, head_weight), "dp", scatter_dimension=0, tiled=True
    )
    targets = target_logits.astype(jnp.float32)
    draft_max, target_max = lax.pmax((jnp.max(logits, axis=1), jnp.max(targets, axis=1)), "vocab")
    draft_total, target_total = lax.psum(
        (
            jnp.sum(jnp.exp(logits - draft_max[:, None]), axis=1),
            jnp.sum(jnp.exp(targets - target_max[:, None]), axis=1),
        ),
        "vocab",
    )
    row_weight = 1048576.0 * live_rows / valid_count
    draft_probs = jnp.exp(logits - draft_max[:, None]) / draft_total[:, None]
    target_probs = jnp.exp(targets - target_max[:, None]) / target_total[:, None]
    logit_grad = (row_weight[:, None] * (draft_probs - target_probs)).astype(jnp.bfloat16)
    partial_grad = jnp.dot(
        lax.all_gather(logit_grad, "dp", axis=0, tiled=True),
        head_weight,
        preferred_element_type=jnp.float32,
    )
    normed_grad = lax.psum(partial_grad, "vocab")
    values = slice_rows.astype(jnp.float32)
    row_dot = lax.psum(jnp.sum(gain_slice * values * normed_grad, axis=1), "dp")
    grad_all = (
        row_factor[:, None] * gain_slice * normed_grad
        - values * (row_factor**3 * row_dot / model_width)[:, None]
    ).astype(jnp.bfloat16)
    grad_share = lax.dynamic_slice_in_dim(grad_all, vocab_index * share_rows, share_rows, 0)
    tree_rows = jnp.arange(group_rows, dtype=jnp.int32) // TREE * TREE + parents
    chosen = jnp.take(features, tree_rows, axis=0)
    grad_joining = lax.dot_general(
        grad_all,
        lax.all_gather(chosen, "dp", axis=0, tiled=True),
        (((0,), (0,)), ((), ())),
        preferred_element_type=jnp.float32,
    )
    return (grad_share, grad_joining)


def solution(mesh):
    placed = (
        P("dp", "vocab"),
        P(),
        P("vocab", "dp"),
        P("dp", "vocab"),
        P("dp"),
        P("dp"),
        P("dp", "vocab"),
    )
    return jax.shard_map(
        body,
        mesh=mesh,
        in_specs=placed,
        out_specs=(P("vocab", "dp"), P("dp", "vocab")),
        check_vma=False,
    )
```

profile of v0, /device:TPU:1, one launch (start us, length us, event | category | flops | bytes accessed | tf_op | source)
XLA Modules:
  0.0 593.1 jit_solution(4355535598762922581)
XLA Ops:
  7.2 0.0 copy-start
  7.2 0.0 all-gather.4.cloned.1.call-start
  7.2 0.7 all-gather.4.cloned.1.call-update
  7.9 77.4 %all-gather.4.cloned.1.call-done = bf16[128,8192]{1,0:T(8,128)(2,1)} async-done(((bf16[128,256]{1,0:T(8,128)(2,1)}), bf16[128,8192]{1,0:T(8,128)(2,1)}) %all-gather.4.cloned.1.call-update) | async-done | bytes 2097168 | tf_op jit(solution)/shard_map/all_gather | solution.py:19
  85.3 0.0 copy-start.4
  85.3 3.2 copy.13
  88.5 8.2 %all-to-all-start = ((bf16[128,8,1024]{2,0,1:T(8,128)(2,1)}), bf16[128,8,1024]{2,0,1:T(8,128)(2,1)S(1)}, u32[]{:S(2)}, u32[]{:S(2)}) async-start(bf16[128,8,1024]{2,0,1:T(8,128)(2,1)} %bitcast.31), calls=%async_computation | async-start | bytes 4194304 | tf_op jit(solution)/shard_map/all_to_all | solution.py:21
  96.7 0.0 reduce-scatter.2.cloned.1.call-start
  96.7 0.7 dynamic_slice.6
  97.4 0.0 copy-done.4
  97.4 0.6 fusion.14
  98.0 24.9 %all-to-all-done = bf16[128,8,1024]{2,0,1:T(8,128)(2,1)S(1)} async-done(((bf16[128,8,1024]{2,0,1:T(8,128)(2,1)}), bf16[128,8,1024]{2,0,1:T(8,128)(2,1)S(1)}, u32[]{:S(2)}, u32[]{:S(2)}) %all-to-all-start) | async-done | bytes 2097184 | tf_op jit(solution)/shard_map/all_to_all | solution.py:21
  122.9 0.5 fusion
  123.4 13.6 %all-reduce.2 = (f32[1024]{0:T(1024)S(1)}, f32[]{:T(128)}) all-reduce(f32[1024]{0:T(1024)S(1)} %bitcast.33, f32[]{:T(128)} %fusion.14), channel_id=1, replica_groups=mesh['dp'=8,'vocab'=32] {'dp'}, use_global_device_ids=true, to_apply=%region_1.0 | all-reduce | flops 1025 | bytes 8200 | tf_op jit(solution)/shard_map/psum | solution.py:28
  137.0 0.0 copy-start.3
  137.0 0.5 fusion.2
  137.5 1.6 copy-done.3
  139.2 6.7 %fusion.15 = f32[1024,2048]{1,0:T(8,128)} fusion(bf16[1024,1024]{1,0:T(8,128)(2,1)S(1)} %fusion.2, bf16[2048,1024]{1,0:T(8,128)(2,1)S(1)} %copy-done.3), kind=kOutput, calls=%fused_computation.37 | convolution fusion | flops 4294967296 | bytes 14680064 | tf_op jit(solution)/shard_map/dot_general | solution.py:10
  145.9 0.0 copy-start.1
  145.9 0.0 reduce-scatter.2.cloned.1.call-update
  145.9 0.0 all-gather.6.cloned.1.call-start
  145.9 1.0 copy-done.1
  146.9 0.2 reduce_max.24
  147.1 0.6 fusion.13
  147.7 50.1 %reduce-scatter.2.cloned.1.call-done = f32[128,2048]{1,0:T(8,128)} async-done(((f32[1024,2048]{1,0:T(8,128)}), f32[128,2048]{1,0:T(8,128)}) %reduce-scatter.2.cloned.1.call-update) | async-done | bytes 1048592 | tf_op jit(solution)/shard_map/reduce_scatter | solution.py:33
  197.8 1.4 reduce_max.23
  199.2 62.2 %all-reduce.1 = (f32[128]{0:T(128)S(1)}, f32[128]{0:T(128)S(1)}) all-reduce(bf16[128]{0:T(256)(128)(2,1)S(1)} %reduce_max.24, f32[128]{0:T(128)S(1)} %reduce_max.23), channel_id=1, replica_groups=mesh['dp'=8,'vocab'=32] {'vocab'}, use_global_device_ids=true, to_apply=%region_10.0 | all-reduce | flops 256 | bytes 1792 | tf_op jit(solution)/shard_map/pmax | solution.py:37
  261.4 1.7 fusion.7
  263.1 55.7 %all-reduce = (f32[128]{0:T(128)S(1)}, f32[128]{0:T(128)S(1)}) all-reduce(f32[128]{0:T(128)S(1)} %get-tuple-element.10, f32[128]{0:T(128)S(1)} %get-tuple-element.11), channel_id=1, replica_groups=mesh['dp'=8,'vocab'=32] {'vocab'}, use_global_device_ids=true, to_apply=%region_12.0 | all-reduce | flops 256 | bytes 2048 | tf_op jit(solution)/shard_map/psum | solution.py:38
  318.8 2.5 multiply_convert_fusion
  321.3 0.0 all-gather.6.cloned.1.call-update
  321.3 0.0 all-reduce.5.cloned.1.call-start
  321.4 58.7 %all-gather.6.cloned.1.call-done = bf16[1024,2048]{1,0:T(8,128)(2,1)} async-done(((bf16[128,2048]{1,0:T(8,128)(2,1)}), bf16[1024,2048]{1,0:T(8,128)(2,1)}) %all-gather.6.cloned.1.call-update) | async-done | bytes 4194320 | tf_op jit(solution)/shard_map/all_gather | solution.py:50
  380.1 9.9 %fusion.16 = f32[1024,1024]{1,0:T(8,128)} fusion(bf16[1024,2048]{1,0:T(8,128)(2,1)} %all-gather.6.cloned.1.call-done, bf16[2048,1024]{1,0:T(8,128)(2,1)} %param.9), kind=kOutput, calls=%fused_computation.38 | convolution fusion | flops 4294967296 | bytes 12582912 | tf_op jit(solution)/shard_map/dot_general | solution.py:49
  390.0 0.0 copy-start.5
  390.0 0.0 all-reduce.5.cloned.1.call-update
  390.0 0.0 all-gather.8.cloned.1.call-start
  390.1 0.6 copy-done.5
  390.7 0.0 copy-done
  390.7 0.9 gather_fusion
  391.6 0.8 broadcast_select_fusion
  392.3 0.0 all-gather.8.cloned.1.call-update
  392.4 158.8 %all-reduce.5.cloned.1.call-done = f32[1024,1024]{1,0:T(8,128)} async-done(((f32[1024,1024]{1,0:T(8,128)}), f32[1024,1024]{1,0:T(8,128)}) %all-reduce.5.cloned.1.call-update) | async-done | bytes 4194320 | tf_op jit(solution)/shard_map/psum | solution.py:54
  551.1 2.8 fusion.4
  553.9 15.7 %psum.47 = f32[1024]{0:T(1024)S(1)} all-reduce(f32[1024]{0:T(1024)S(1)} %fusion.4), channel_id=1, replica_groups=mesh['dp'=8,'vocab'=32] {'dp'}, use_global_device_ids=true, to_apply=%region_15.0 | all-reduce | flops 1024 | bytes 8192 | tf_op jit(solution)/shard_map/psum | solution.py:56
  569.6 3.1 fusion.6
  572.7 0.0 copy-start.2
  572.7 1.3 copy-done.2
  574.0 0.6 constant_dynamic-slice_fusion
  574.7 6.3 %all-gather.8.cloned.1.call-done = bf16[1024,768]{1,0:T(8,128)(2,1)} async-done(((bf16[128,768]{1,0:T(8,128)(2,1)}), bf16[1024,768]{1,0:T(8,128)(2,1)}) %all-gather.8.cloned.1.call-update) | async-done | bytes 1572880 | tf_op jit(solution)/shard_map/all_gather | solution.py:66
  581.0 5.6 fusion.17
  (4 shorter events, 0.0 us)
Async XLA Ops:
  7.2 383.5 %copy-start = (bf16[128,768]{1,0:T(8,128)(2,1)S(1)}, bf16[128,768]{1,0:T(8,128)(2,1)}, u32[]{:S(2)}) copy-start(bf16[128,768]{1,0:T(8,128)(2,1)} %param.13) | copy-start | bytes 589828
  7.2 78.1 %all-gather.4.cloned.1.call-start = ((), (), s32[]{:S(2)}) async-start(), calls=%async_computation.2 | async-start | bytes 2162688 | tf_op jit(solution)/shard_map/all_gather | solution.py:19
  85.3 12.1 %copy-start.4 = (s32[128]{0:T(128)S(1)}, s32[128]{0:T(128)}, u32[]{:S(2)}) copy-start(s32[128]{0:T(128)} %param.11) | copy-start | bytes 1540
  88.5 34.4 %all-to-all-start = ((bf16[128,8,1024]{2,0,1:T(8,128)(2,1)}), bf16[128,8,1024]{2,0,1:T(8,128)(2,1)S(1)}, u32[]{:S(2)}, u32[]{:S(2)}) async-start(bf16[128,8,1024]{2,0,1:T(8,128)(2,1)} %bitcast.31), calls=%async_computation | async-start | bytes 4194304 | tf_op jit(solution)/shard_map/all_to_all | solution.py:21
  96.7 101.1 %reduce-scatter.2.cloned.1.call-start = ((), (), s32[]{:S(2)}) async-start(), calls=%async_computation.3 | async-start | bytes 9437184 | tf_op jit(solution)/shard_map/reduce_scatter | solution.py:33
  137.0 2.2 copy-start.3
  145.9 1.0 copy-start.1
  145.9 234.2 %all-gather.6.cloned.1.call-start = ((), (), s32[]{:S(2)}) async-start(), calls=%async_computation.4 | async-start | bytes 4718592 | tf_op jit(solution)/shard_map/all_gather | solution.py:50
  321.3 229.8 %all-reduce.5.cloned.1.call-start = ((), (), s32[]{:S(2)}) async-start(), calls=%async_computation.5 | async-start | bytes 8388608 | tf_op jit(solution)/shard_map/psum | solution.py:54
  390.0 0.7 copy-start.5
  390.0 191.0 %all-gather.8.cloned.1.call-start = ((), (), s32[]{:S(2)}) async-start(), calls=%async_computation.6 | async-start | bytes 1769472 | tf_op jit(solution)/shard_map/all_gather | solution.py:66
  572.7 1.4 copy-start.2
Sparse Core Ops, SparseCore 0:
  10.5 74.8 all-gather.3
  146.0 51.7 reduce-scatter.1
  321.5 58.6 all-gather.5
  390.1 160.9 all-reduce.4
  553.4 27.5 all-gather.7
where the time goes:
time: 594 us; the launch traced here: 593 us
  waiting for transfers between devices  377 us (63%)
  blocking collectives  147 us (25%)
  matrix products  22.2 us (4%)
  other arithmetic  14.6 us (2%)
  between operations  13.9 us (2%)
  local copies, waits for them, and re-layouts  9.89 us (2%)
  starting transfers between devices  8.38 us (1%)
    psum x1, waiting for transfers between devices, body(): normed_grad = lax.psum(partial_grad, 'vocab')  159 us
    all_gather x1, waiting for transfers between devices, body(): whole_rows = lax.all_gather(hidden, 'vocab', axis=1, tiled=True)  77.4 us
    pmax x1, blocking collectives, body(): lax.pmax((jnp.max(logits, axis=1), jnp.max(targets, axis=1)), 'vocab')  62.2 us
    all_gather x1, waiting for transfers between devices, body(): lax.all_gather(logit_grad, 'dp', axis=0, tiled=True)  58.7 us
    psum x1, blocking collectives, body(): lax.psum((jnp.sum(jnp.exp(logits - draft_max[:, None]), axis=1), jnp.sum(...  55.7 us
    reduce_scatter x1, waiting for transfers between devices, body(): lax.psum_scatter(row_logits(normed, head_weight), 'dp', scatter_dimension...  50.1 us
    all_to_all x1, waiting for transfers between devices, body(): lax.all_to_all(whole_rows, 'dp', split_axis=1, concat_axis=0, tiled=True)  24.9 us
    psum x1, blocking collectives, body(): row_dot = lax.psum(jnp.sum(gain_slice * values * normed_grad, axis=1), 'dp')  15.7 us
  transfers between devices with their start and end apart: 6, of which 6 were waited for; matrix products, arithmetic and copies ran while one was open for 2% of the time, Pallas kernels for 0%

commit v1 on v0

--- a/solution.py
+++ b/solution.py
@@ -51,7 +51,11 @@
         head_weight,
         preferred_element_type=jnp.float32,
     )
-    normed_grad = lax.psum(partial_grad, "vocab")
+    normed_grad = partial_grad
+    for hop in (1, 2, 4, 8, 16):
+        normed_grad = normed_grad + lax.ppermute(
+            normed_grad, "vocab", [(dev, dev ^ hop) for dev in range(32)]
+        )
     values = slice_rows.astype(jnp.float32)
     row_dot = lax.psum(jnp.sum(gain_slice * values * normed_grad, axis=1), "dp")
     grad_all = (

time: 594 us -> 1080 us (1.82)
  waiting for transfers between devices: 377 us -> 841 us
  starting transfers between devices: 8.38 us -> 22.7 us
    ppermute x0 -> x5, waiting for transfers between devices: none -> 629 us  [body(): lax.ppermute(normed_grad, 'vocab', [(dev, dev ^ hop) for dev in range(32)])]
    psum x1 -> x0, waiting for transfers between devices: 159 us -> none  [body(): normed_grad = lax.psum(partial_grad, 'vocab')]
    ppermute x0 -> x5, starting transfers between devices: none -> 14.4 us  [body(): lax.ppermute(normed_grad, 'vocab', [(dev, dev ^ hop) for dev in range(32)])]
  transfers between devices with their start and end apart: 6 -> 10, of which waited for: 6 -> 9; matrix products, arithmetic and copies ran while one was open for 2% -> 1% of each run, Pallas kernels for 0% -> 0%
where the time goes in v1:
time: 1080 us; the launch traced here: 1070 us
  waiting for transfers between devices  841 us (78%)
  blocking collectives  145 us (13%)
  other arithmetic  24 us (2%)
  starting transfers between devices  22.7 us (2%)
  matrix products  19.8 us (2%)
  between operations  13.9 us (1%)
    ppermute x5, waiting for transfers between devices, body(): lax.ppermute(normed_grad, 'vocab', [(dev, dev ^ hop) for dev in range(32)])  629 us
    all_gather x1, waiting for transfers between devices, body(): whole_rows = lax.all_gather(hidden, 'vocab', axis=1, tiled=True)  77.4 us
    pmax x1, blocking collectives, body(): lax.pmax((jnp.max(logits, axis=1), jnp.max(targets, axis=1)), 'vocab')  62.2 us
    all_gather x1, waiting for transfers between devices, body(): lax.all_gather(logit_grad, 'dp', axis=0, tiled=True)  58.7 us
    psum x1, blocking collectives, body(): lax.psum((jnp.sum(jnp.exp(logits - draft_max[:, None]), axis=1), jnp.sum(...  55.7 us
    reduce_scatter x1, waiting for transfers between devices, body(): lax.psum_scatter(row_logits(normed, head_weight), 'dp', scatter_dimension...  50.1 us
    all_to_all x1, waiting for transfers between devices, body(): lax.all_to_all(whole_rows, 'dp', split_axis=1, concat_axis=0, tiled=True)  24.9 us
  transfers between devices with their start and end apart: 10, of which 9 were waited for; matrix products, arithmetic and copies ran while one was open for 1% of the time, Pallas kernels for 0%

profile of v1, /device:TPU:1, one launch (start us, length us, event | category | flops | bytes accessed | tf_op | source)
XLA Modules:
  0.0 1075.0 jit_solution(12671591084533924796)
XLA Ops:
  7.2 0.0 copy-start
  7.2 0.0 all-gather.4.cloned.1.call-start
  7.2 0.7 all-gather.4.cloned.1.call-update
  7.9 77.4 %all-gather.4.cloned.1.call-done = bf16[128,8192]{1,0:T(8,128)(2,1)} async-done(((bf16[128,256]{1,0:T(8,128)(2,1)}), bf16[128,8192]{1,0:T(8,128)(2,1)}) %all-gather.4.cloned.1.call-update) | async-done | bytes 2097168 | tf_op jit(solution)/shard_map/all_gather | solution.py:19
  85.3 0.0 copy-start.4
  85.3 3.2 copy.13
  88.5 8.2 all-to-all-start
  96.7 0.0 reduce-scatter.2.cloned.1.call-start
  96.7 0.7 dynamic_slice.6
  97.4 0.0 copy-done.4
  97.4 0.6 fusion.14
  98.0 24.9 %all-to-all-done = bf16[128,8,1024]{2,0,1:T(8,128)(2,1)S(1)} async-done(((bf16[128,8,1024]{2,0,1:T(8,128)(2,1)}), bf16[128,8,1024]{2,0,1:T(8,128)(2,1)S(1)}, u32[]{:S(2)}, u32[]{:S(2)}) %all-to-all-start) | async-done | bytes 2097184 | tf_op jit(solution)/shard_map/all_to_all | solution.py:21
  122.9 0.5 fusion
  123.4 13.6 %all-reduce.2 = (f32[1024]{0:T(1024)S(1)}, f32[]{:T(128)}) all-reduce(f32[1024]{0:T(1024)S(1)} %bitcast.33, f32[]{:T(128)} %fusion.14), channel_id=1, replica_groups=mesh['dp'=8,'vocab'=32] {'dp'}, use_global_device_ids=true, to_apply=%region_1.0 | all-reduce | flops 1025 | bytes 8200 | tf_op jit(solution)/shard_map/psum | solution.py:28
  137.0 0.0 copy-start.3
  137.0 0.5 fusion.2
  137.5 1.6 copy-done.3
  139.2 6.7 fusion.15
  145.9 0.0 copy-start.1
  145.9 0.0 reduce-scatter.2.cloned.1.call-update
  145.9 0.0 all-gather.6.cloned.1.call-start
  145.9 1.0 copy-done.1
  146.9 0.2 reduce_max.24
  147.1 0.6 fusion.13
  147.7 50.1 %reduce-scatter.2.cloned.1.call-done = f32[128,2048]{1,0:T(8,128)} async-done(((f32[1024,2048]{1,0:T(8,128)}), f32[128,2048]{1,0:T(8,128)}) %reduce-scatter.2.cloned.1.call-update) | async-done | bytes 1048592 | tf_op jit(solution)/shard_map/reduce_scatter | solution.py:33
  197.8 1.4 reduce_max.23
  199.2 62.2 %all-reduce.1 = (f32[128]{0:T(128)S(1)}, f32[128]{0:T(128)S(1)}) all-reduce(bf16[128]{0:T(256)(128)(2,1)S(1)} %reduce_max.24, f32[128]{0:T(128)S(1)} %reduce_max.23), channel_id=1, replica_groups=mesh['dp'=8,'vocab'=32] {'vocab'}, use_global_device_ids=true, to_apply=%region_10.0 | all-reduce | flops 256 | bytes 1792 | tf_op jit(solution)/shard_map/pmax | solution.py:37
  261.4 1.7 fusion.7
  263.1 55.7 %all-reduce = (f32[128]{0:T(128)S(1)}, f32[128]{0:T(128)S(1)}) all-reduce(f32[128]{0:T(128)S(1)} %get-tuple-element.10, f32[128]{0:T(128)S(1)} %get-tuple-element.11), channel_id=1, replica_groups=mesh['dp'=8,'vocab'=32] {'vocab'}, use_global_device_ids=true, to_apply=%region_12.0 | all-reduce | flops 256 | bytes 2048 | tf_op jit(solution)/shard_map/psum | solution.py:38
  318.8 2.5 multiply_convert_fusion
  321.3 0.0 all-gather.6.cloned.1.call-update
  321.4 0.0 all-gather.8.cloned.1.call-start
  321.4 58.7 %all-gather.6.cloned.1.call-done = bf16[1024,2048]{1,0:T(8,128)(2,1)} async-done(((bf16[128,2048]{1,0:T(8,128)(2,1)}), bf16[1024,2048]{1,0:T(8,128)(2,1)}) %all-gather.6.cloned.1.call-update) | async-done | bytes 4194320 | tf_op jit(solution)/shard_map/all_gather | solution.py:50
  380.1 7.5 fusion.16
  387.6 1.3 collective-permute-start
  388.9 90.6 %collective-permute-done = f32[1024,1024]{1,0:T(8,128)S(1)} collective-permute-done((f32[1024,1024]{1,0:T(8,128)S(1)}, f32[1024,1024]{1,0:T(8,128)S(1)}, u32[]{:S(2)}, u32[]{:S(2)}) %collective-permute-start) | collective-permute-done | bytes 4194336 | tf_op jit(solution)/shard_map/ppermute | solution.py:56
  479.6 1.4 add.54
  480.9 2.8 collective-permute-start.1
  483.8 89.7 %collective-permute-done.1 = f32[1024,1024]{1,0:T(8,128)S(1)} collective-permute-done((f32[1024,1024]{1,0:T(8,128)S(1)}, f32[1024,1024]{1,0:T(8,128)S(1)}, u32[]{:S(2)}, u32[]{:S(2)}) %collective-permute-start.1) | collective-permute-done | bytes 4194336 | tf_op jit(solution)/shard_map/ppermute | solution.py:56
  573.5 1.4 add.55
  574.9 1.4 collective-permute-start.2
  576.3 88.8 %collective-permute-done.2 = f32[1024,1024]{1,0:T(8,128)S(1)} collective-permute-done((f32[1024,1024]{1,0:T(8,128)S(1)}, f32[1024,1024]{1,0:T(8,128)S(1)}, u32[]{:S(2)}, u32[]{:S(2)}) %collective-permute-start.2) | collective-permute-done | bytes 4194336 | tf_op jit(solution)/shard_map/ppermute | solution.py:56
  665.1 1.4 add.56
  666.5 0.0 copy-start.5
  666.5 2.5 collective-permute-start.3
  669.0 180.0 %collective-permute-done.3 = f32[1024,1024]{1,0:T(8,128)S(1)} collective-permute-done((f32[1024,1024]{1,0:T(8,128)S(1)}, f32[1024,1024]{1,0:T(8,128)S(1)}, u32[]{:S(2)}, u32[]{:S(2)}) %collective-permute-start.3) | collective-permute-done | bytes 4194336 | tf_op jit(solution)/shard_map/ppermute | solution.py:56
  849.0 2.9 add.57
  851.9 6.3 collective-permute-start.4
  858.2 0.0 copy-done.5
  858.2 0.0 copy-done
  858.2 0.9 gather_fusion
  859.1 0.8 broadcast_select_fusion
  859.9 0.0 all-gather.8.cloned.1.call-update
  859.9 179.4 %collective-permute-done.4 = f32[1024,1024]{1,0:T(8,128)} collective-permute-done((f32[1024,1024]{1,0:T(8,128)}, f32[1024,1024]{1,0:T(8,128)}, u32[]{:S(2)}, u32[]{:S(2)}) %collective-permute-start.4) | collective-permute-done | bytes 4194336 | tf_op jit(solution)/shard_map/ppermute | solution.py:56
  1039.4 4.2 fusion.4
  1043.6 13.3 %psum.39 = f32[1024]{0:T(1024)S(1)} all-reduce(f32[1024]{0:T(1024)S(1)} %fusion.4), channel_id=1, replica_groups=mesh['dp'=8,'vocab'=32] {'dp'}, use_global_device_ids=true, to_apply=%region_14.0 | all-reduce | flops 1024 | bytes 8192 | tf_op jit(solution)/shard_map/psum | solution.py:60
  1056.8 4.1 fusion.6
  1060.9 0.0 copy-start.2
  1060.9 1.3 copy-done.2
  1062.3 0.6 constant_dynamic-slice_fusion
  1062.9 0.0 all-gather.8.cloned.1.call-done
  1062.9 5.6 fusion.17
  (4 shorter events, 0.0 us)
Async XLA Ops:
  7.2 851.1 %copy-start = (bf16[128,768]{1,0:T(8,128)(2,1)S(1)}, bf16[128,768]{1,0:T(8,128)(2,1)}, u32[]{:S(2)}) copy-start(bf16[128,768]{1,0:T(8,128)(2,1)} %param.13) | copy-start | bytes 589828
  7.2 78.1 %all-gather.4.cloned.1.call-start = ((), (), s32[]{:S(2)}) async-start(), calls=%async_computation.2 | async-start | bytes 2162688 | tf_op jit(solution)/shard_map/all_gather | solution.py:19
  85.3 12.1 %copy-start.4 = (s32[128]{0:T(128)S(1)}, s32[128]{0:T(128)}, u32[]{:S(2)}) copy-start(s32[128]{0:T(128)} %param.11) | copy-start | bytes 1540
  88.5 34.4 %all-to-all-start = ((bf16[128,8,1024]{2,0,1:T(8,128)(2,1)}), bf16[128,8,1024]{2,0,1:T(8,128)(2,1)S(1)}, u32[]{:S(2)}, u32[]{:S(2)}) async-start(bf16[128,8,1024]{2,0,1:T(8,128)(2,1)} %bitcast.31), calls=%async_computation | async-start | bytes 4194304 | tf_op jit(solution)/shard_map/all_to_all | solution.py:21
  96.7 101.1 %reduce-scatter.2.cloned.1.call-start = ((), (), s32[]{:S(2)}) async-start(), calls=%async_computation.3 | async-start | bytes 9437184 | tf_op jit(solution)/shard_map/reduce_scatter | solution.py:33
  137.0 2.2 copy-start.3
  145.9 1.0 copy-start.1
  145.9 234.2 %all-gather.6.cloned.1.call-start = ((), (), s32[]{:S(2)}) async-start(), calls=%async_computation.4 | async-start | bytes 4718592 | tf_op jit(solution)/shard_map/all_gather | solution.py:50
  321.4 741.5 %all-gather.8.cloned.1.call-start = ((), (), s32[]{:S(2)}) async-start(), calls=%async_computation.5 | async-start | bytes 1769472 | tf_op jit(solution)/shard_map/all_gather | solution.py:70
  387.6 91.9 %collective-permute-start = (f32[1024,1024]{1,0:T(8,128)S(1)}, f32[1024,1024]{1,0:T(8,128)S(1)}, u32[]{:S(2)}, u32[]{:S(2)}) collective-permute-start(f32[1024,1024]{1,0:T(8,128)S(1)} %fusion.16), channel_id=1, source_target_pairs={{0,1},{1,0},{2,3},{3,2},{4,5},{5,4},{6,7},{7,6},{8,9},{9,8},{10,11... | collective-permute-start | bytes 12582920 | tf_op jit(solution)/shard_map/ppermute | solution.py:56
  480.9 92.6 %collective-permute-start.1 = (f32[1024,1024]{1,0:T(8,128)S(1)}, f32[1024,1024]{1,0:T(8,128)S(1)}, u32[]{:S(2)}, u32[]{:S(2)}) collective-permute-start(f32[1024,1024]{1,0:T(8,128)S(1)} %add.54), channel_id=1, source_target_pairs={{0,2},{1,3},{2,0},{3,1},{4,6},{5,7},{6,4},{7,5},{8,10},{9,11},{10,... | collective-permute-start | bytes 12582920 | tf_op jit(solution)/shard_map/ppermute | solution.py:56
  574.9 90.2 %collective-permute-start.2 = (f32[1024,1024]{1,0:T(8,128)S(1)}, f32[1024,1024]{1,0:T(8,128)S(1)}, u32[]{:S(2)}, u32[]{:S(2)}) collective-permute-start(f32[1024,1024]{1,0:T(8,128)S(1)} %add.55), channel_id=1, source_target_pairs={{0,4},{1,5},{2,6},{3,7},{4,0},{5,1},{6,2},{7,3},{8,12},{9,13},{10,... | collective-permute-start | bytes 12582920 | tf_op jit(solution)/shard_map/ppermute | solution.py:56
  666.5 191.7 %copy-start.5 = (s32[128]{0:T(128)S(1)}, s32[128]{0:T(128)}, u32[]{:S(2)}) copy-start(s32[128]{0:T(128)} %param.12) | copy-start | bytes 1540
  666.5 182.5 %collective-permute-start.3 = (f32[1024,1024]{1,0:T(8,128)S(1)}, f32[1024,1024]{1,0:T(8,128)S(1)}, u32[]{:S(2)}, u32[]{:S(2)}) collective-permute-start(f32[1024,1024]{1,0:T(8,128)S(1)} %add.56), channel_id=1, source_target_pairs={{0,8},{1,9},{2,10},{3,11},{4,12},{5,13},{6,14},{7,15},{8,0},{9,1},... | collective-permute-start | bytes 12582920 | tf_op jit(solution)/shard_map/ppermute | solution.py:56
  851.9 187.5 %collective-permute-start.4 = (f32[1024,1024]{1,0:T(8,128)}, f32[1024,1024]{1,0:T(8,128)}, u32[]{:S(2)}, u32[]{:S(2)}) collective-permute-start(f32[1024,1024]{1,0:T(8,128)} %add.57), channel_id=1, source_target_pairs={{0,16},{1,17},{2,18},{3,19},{4,20},{5,21},{6,22},{7,23},{8,24},{9,... | collective-permute-start | bytes 12582920 | tf_op jit(solution)/shard_map/ppermute | solution.py:56
  1060.9 1.4 copy-start.2
Sparse Core Ops, SparseCore 0:
  10.5 74.8 all-gather.3
  146.0 51.7 reduce-scatter.1
  321.5 58.6 all-gather.5
  860.0 22.4 all-gather.7
